TPU v7x, 256 devices: a whole 4x4x8 slice. The times are simulated.
256 devices in a mesh: blk: 64 (over z, x, y_hi), aux: 4 (over y_lo, core).
Axes of the slice: x: 4, y: 4 (y_hi: 2, y_lo: 2; y = y_hi * 2 + y_lo), z: 8, core: 2. Of those that a mesh axis runs over, the one named last changes fastest.
Arguments:
- coeffs: bfloat16 [16384, 512], P('blk'), may hold values from -6 to 6
- fitting: bfloat16 [16384, 256, 256], P('blk', 'aux'), may hold values from -0.375 to 0.375
- screen: int32 [256, 4], P('blk'), may hold values from 0 to 255, as said below
- counts: int32 [256], P('blk'), may hold values from 1 to 4, as said below
- tile_order: int32 [64, 16], P('blk'), may hold values from 0 to 15, each once within a row
Outputs:
- fock_tiles: float32 [1024, 4096], P(('blk', 'aux'))
Inputs may be any that keep to these rules, and one draw needn't show every extreme that they name: `screen`: each partner block lies on the same index of blk as its basis block or on one of the two indices before or after it, counted around the axis. `counts`: some block uses all 4 slots and some block only one.
All inputs are finite; a program needn't handle non-finite values.
Results may differ from a plain program's by a relative error of at most 0.0003.
Values may be sent and summed in bfloat16 or wider, within the bound.
A program may use at most 128 MiB of HBM per device.

v0:
```python
import jax
import jax.numpy as jnp
from jax import lax
from jax.sharding import PartitionSpec as P


def passed_along(value, axis, by):
    length = lax.axis_size(axis)
    return lax.ppermute(value, axis, [(i, (i + by) % length) for i in range(length)])


def per_device(coeffs, fitting, screen, counts, tile_order):
    blocks_here = screen.shape[0]
    slot_count = screen.shape[1]
    block_width = coeffs.shape[0] // blocks_here
    orbitals = coeffs.shape[1]
    aux_here = fitting.shape[1]
    loop_size = lax.axis_size("blk")
    position = lax.axis_index("blk")
    earlier = []
    later = []
    moving_up = coeffs
    moving_down = coeffs
    for step in range(2):
        moving_up = passed_along(moving_up, "blk", 1)
        earlier.append(moving_up)
        moving_down = passed_along(moving_down, "blk", -1)
        later.append(moving_down)
    pieces = [earlier[1], earlier[0], coeffs, later[0], later[1]]
    window = jnp.concatenate(pieces, axis=0).reshape(5 * blocks_here, block_width, orbitals)
    owner = screen // blocks_here
    distance = (owner - position + loop_size) % loop_size
    distance = jnp.where(distance > loop_size // 2, distance - loop_size, distance)
    local_block = (distance + 2) * blocks_here + screen % blocks_here
    slot_index = jnp.arange(slot_count, dtype=jnp.int32)
    keep_slot = slot_index[None, :] < counts[:, None]
    picked = jnp.where(
        keep_slot[:, :, None, None], window[local_block], jnp.zeros((), jnp.bfloat16)
    )
    picked = picked.reshape(blocks_here, slot_count * block_width, orbitals)
    fit_blocks = fitting.reshape(blocks_here, block_width, aux_here, slot_count * block_width)
    half = jnp.einsum(
        "mupl,mli->mupi", fit_blocks, picked, preferred_element_type=jnp.float32
    ).astype(jnp.bfloat16)
    flat = half.reshape(blocks_here * block_width, aux_here * orbitals)
    total_aux = aux_here * lax.axis_size("aux")
    gram = lax.dot_general(flat, flat, (((1,), (1,)), ((), ())), preferred_element_type=jnp.float32)
    gram = gram / jnp.sqrt(jnp.float32(total_aux * orbitals))
    tiles = gram.reshape(blocks_here, block_width, blocks_here, block_width).transpose(0, 2, 1, 3)
    tiles = tiles.reshape(blocks_here * blocks_here, block_width * block_width)
    ordered = tiles[tile_order[0]]
    share = ordered.shape[0] // lax.axis_size("aux")
    summed = lax.psum(ordered, "aux")
    return lax.dynamic_slice_in_dim(summed, lax.axis_index("aux") * share, share, 0)


def solution(mesh):
    placed = (P("blk", None), P("blk", "aux", None), P("blk", None), P("blk"), P("blk", None))
    return jax.shard_map(
        per_device, mesh=mesh, in_specs=placed, out_specs=P(("blk", "aux"), None), check_vma=False
    )
```

profile of v0, /device:TPU:1, one launch (start us, length us, event | category | flops | bytes accessed | tf_op | source)
XLA Modules:
  0.0 137.2 jit_solution(14247176783398623179)
XLA Ops:
  6.5 0.0 all-reduce.2.cloned.1.call-start
  6.5 3.7 %collective-permute-start = (bf16[256,512]{1,0:T(8,128)(2,1)}, bf16[256,512]{1,0:T(8,128)(2,1)S(1)}, u32[]{:S(2)}, u32[]{:S(2)}) collective-permute-start(bf16[256,512]{1,0:T(8,128)(2,1)} %param.5), channel_id=1, source_target_pairs={{0,4},{4,8},{8,12},{12,16},{16,20},{20,24},{24,28},{28,32},{32,36}... | collective-permute-start | bytes 786440 | tf_op jit(solution)/shard_map/ppermute | solution.py:9
  10.3 7.5 %collective-permute-start.2 = (bf16[256,512]{1,0:T(8,128)(2,1)}, bf16[256,512]{1,0:T(8,128)(2,1)S(1)}, u32[]{:S(2)}, u32[]{:S(2)}) collective-permute-start(bf16[256,512]{1,0:T(8,128)(2,1)} %param.5), channel_id=1, source_target_pairs={{0,252},{4,0},{8,4},{12,8},{16,12},{20,16},{24,20},{28,24},{32,28}... | collective-permute-start | bytes 786440 | tf_op jit(solution)/shard_map/ppermute | solution.py:9
  17.8 0.7 iota_compare_fusion
  18.5 0.7 compare_select_fusion
  19.2 4.8 %collective-permute-done = bf16[256,512]{1,0:T(8,128)(2,1)S(1)} collective-permute-done((bf16[256,512]{1,0:T(8,128)(2,1)}, bf16[256,512]{1,0:T(8,128)(2,1)S(1)}, u32[]{:S(2)}, u32[]{:S(2)}) %collective-permute-start) | collective-permute-done | bytes 262176 | tf_op jit(solution)/shard_map/ppermute | solution.py:9
  24.0 0.8 collective-permute-start.1
  24.8 0.7 fusion.8
  25.4 0.1 reshape.74
  25.5 0.1 broadcast_in_dim.23
  25.6 0.1 broadcast_in_dim.24
  25.7 0.0 collective-permute-done.2
  25.7 7.6 %collective-permute-start.3 = (bf16[256,512]{1,0:T(8,128)(2,1)S(1)}, bf16[256,512]{1,0:T(8,128)(2,1)S(1)}, u32[]{:S(2)}, u32[]{:S(2)}) collective-permute-start(bf16[256,512]{1,0:T(8,128)(2,1)S(1)} %collective-permute-done.2), channel_id=1, source_target_pairs={{0,252},{4,0},{8,4},{12,8},{16,12},{20,16},{24,20},{28,24},{32,28}... | collective-permute-start | bytes 786440 | tf_op jit(solution)/shard_map/ppermute | solution.py:9
  33.3 4.1 %collective-permute-done.1 = bf16[256,512]{1,0:T(8,128)(2,1)S(1)} collective-permute-done((bf16[256,512]{1,0:T(8,128)(2,1)S(1)}, bf16[256,512]{1,0:T(8,128)(2,1)S(1)}, u32[]{:S(2)}, u32[]{:S(2)}) %collective-permute-start.1) | collective-permute-done | bytes 262176 | tf_op jit(solution)/shard_map/ppermute | solution.py:9
  37.4 1.0 constant_dynamic-update-slice_fusion.2
  38.4 0.0 collective-permute-done.3
  38.4 0.6 gather_fusion
  39.1 0.2 bitcast_select_fusion
  39.3 11.6 %convolution_convert_fusion = bf16[4,512,64,64]{1,3,2,0:T(8,128)(2,1)} fusion(bf16[4,64,64,256]{3,2,1,0:T(8,128)(2,1)} %bitcast.29, bf16[4,256,512]{2,1,0:T(8,128)(2,1)S(1)} %bitcast_select_fusion), kind=kOutput, calls=%fused_computation.2 | convolution fusion | flops 4303355904 | bytes 26214400 | tf_op jit(solution)/shard_map/mupl,mli->mupi/dot_general | solution.py:42
  50.9 18.4 %copy.8 = bf16[32,8,64,512]{3,1,2,0:T(8,128)(2,1)} copy(bf16[32,8,64,512]{3,2,1,0:T(8,128)(2,1)} %bitcast.24) | data formatting | bytes 33554432
  69.3 12.9 %convolution_multiply_fusion = f32[256,256]{1,0:T(8,128)S(1)} fusion(bf16[256,32768]{1,0:T(8,128)(2,1)} %bitcast.25), kind=kOutput, calls=%fused_computation.3 | convolution fusion | flops 4295032832 | bytes 17039360 | tf_op jit(solution)/shard_map/dot_general | solution.py:47
  82.2 0.2 reshape.70
  82.5 0.1 copy.6
  82.6 0.2 reshape.71
  82.7 1.3 gather_fusion.1
  84.1 0.0 all-reduce.2.cloned.1.call-update
  84.1 44.7 %all-reduce.2.cloned.1.call-done = f32[16,4096]{1,0:T(8,128)} async-done(((f32[16,4096]{1,0:T(8,128)}), f32[16,4096]{1,0:T(8,128)}) %all-reduce.2.cloned.1.call-update) | async-done | bytes 262160 | tf_op jit(solution)/shard_map/psum | solution.py:53
  128.8 1.5 %constant_dynamic-slice_fusion = f32[4,4096]{1,0:T(4,128)} fusion(f32[16,4096]{1,0:T(8,128)} %all-reduce.2.cloned.1.call-done, s32[]{:T(128)S(6)} %select_n.47), kind=kLoop, calls=%fused_computation.34 | loop fusion | bytes 131076 | tf_op jit(solution)/shard_map/dynamic_slice | solution.py:54
  (6 shorter events, 0.1 us)
Async XLA Ops:
  6.5 122.2 %all-reduce.2.cloned.1.call-start = ((), (), s32[]{:S(2)}) async-start(), calls=%async_computation | async-start | bytes 524288 | tf_op jit(solution)/shard_map/psum | solution.py:53
  6.5 17.5 %collective-permute-start = (bf16[256,512]{1,0:T(8,128)(2,1)}, bf16[256,512]{1,0:T(8,128)(2,1)S(1)}, u32[]{:S(2)}, u32[]{:S(2)}) collective-permute-start(bf16[256,512]{1,0:T(8,128)(2,1)} %param.5), channel_id=1, source_target_pairs={{0,4},{4,8},{8,12},{12,16},{16,20},{20,24},{24,28},{28,32},{32,36}... | collective-permute-start | bytes 786440 | tf_op jit(solution)/shard_map/ppermute | solution.py:9
  10.3 15.4 %collective-permute-start.2 = (bf16[256,512]{1,0:T(8,128)(2,1)}, bf16[256,512]{1,0:T(8,128)(2,1)S(1)}, u32[]{:S(2)}, u32[]{:S(2)}) collective-permute-start(bf16[256,512]{1,0:T(8,128)(2,1)} %param.5), channel_id=1, source_target_pairs={{0,252},{4,0},{8,4},{12,8},{16,12},{20,16},{24,20},{28,24},{32,28}... | collective-permute-start | bytes 786440 | tf_op jit(solution)/shard_map/ppermute | solution.py:9
  24.0 13.3 %collective-permute-start.1 = (bf16[256,512]{1,0:T(8,128)(2,1)S(1)}, bf16[256,512]{1,0:T(8,128)(2,1)S(1)}, u32[]{:S(2)}, u32[]{:S(2)}) collective-permute-start(bf16[256,512]{1,0:T(8,128)(2,1)S(1)} %collective-permute-done), channel_id=1, source_target_pairs={{0,4},{4,8},{8,12},{12,16},{16,20},{20,24},{24,28},{28,32},{32,36}... | collective-permute-start | bytes 786440 | tf_op jit(solution)/shard_map/ppermute | solution.py:9
  25.7 12.7 %collective-permute-start.3 = (bf16[256,512]{1,0:T(8,128)(2,1)S(1)}, bf16[256,512]{1,0:T(8,128)(2,1)S(1)}, u32[]{:S(2)}, u32[]{:S(2)}) collective-permute-start(bf16[256,512]{1,0:T(8,128)(2,1)S(1)} %collective-permute-done.2), channel_id=1, source_target_pairs={{0,252},{4,0},{8,4},{12,8},{16,12},{20,16},{24,20},{28,24},{32,28}... | collective-permute-start | bytes 786440 | tf_op jit(solution)/shard_map/ppermute | solution.py:9
Sparse Core Ops, SparseCore 0:
  84.2 44.5 all-reduce.1
where the time goes:
time: 138 us; the launch traced here: 137 us
  waiting for transfers between devices  53.6 us (39%)
  matrix products  24.5 us (18%)
  local copies, waits for them, and re-layouts  23.7 us (17%)
  starting transfers between devices  19.6 us (14%)
  between operations  13.5 us (10%)
  other arithmetic  2.3 us (2%)
    psum x1, waiting for transfers between devices, per_device(): summed = lax.psum(ordered, 'aux')  44.7 us
    ppermute x4, starting transfers between devices, passed_along(): lax.ppermute(value, axis, [(i, (i + by) % length) for i in range(length)])  19.6 us
    unnamed x5, local copies, waits for them, and re-layouts  19.5 us
    dot_general x1, matrix products, per_device(): lax.dot_general(flat, flat, (((1,), (1,)), ((), ())), preferred_element_t...  12.9 us
    dot_general x1, matrix products, per_device(): jnp.einsum('mupl,mli->mupi', fit_blocks, picked, preferred_element_type=j...  11.6 us
    ppermute x4, waiting for transfers between devices, passed_along(): lax.ppermute(value, axis, [(i, (i + by) % length) for i in range(length)])  8.87 us
  transfers between devices with their start and end apart: 5, of which 3 were waited for; matrix products, arithmetic and copies ran while one was open for 2% of the time, Pallas kernels for 0%

commit v1 on v0

--- a/solution.py
+++ b/solution.py
@@ -2,6 +2,12 @@
 import jax.numpy as jnp
 from jax import lax
 from jax.sharding import PartitionSpec as P
+
+
+def add_all(value, axis):
+    parts = lax.all_gather(value, axis, axis=0, tiled=False)
+    total = parts.sum(axis=0)
+    return total
 
 
 def passed_along(value, axis, by):
@@ -50,7 +56,7 @@
     tiles = tiles.reshape(blocks_here * blocks_here, block_width * block_width)
     ordered = tiles[tile_order[0]]
     share = ordered.shape[0] // lax.axis_size("aux")
-    summed = lax.psum(ordered, "aux")
+    summed = add_all(ordered, "aux")
     return lax.dynamic_slice_in_dim(summed, lax.axis_index("aux") * share, share, 0)
 
 

time: 138 us -> 120 us (0.87)
  waiting for transfers between devices: 53.6 us -> 35.4 us
    psum x1 -> x0, waiting for transfers between devices: 44.7 us -> none  [per_device(): summed = lax.psum(ordered, 'aux')]
    all_gather x0 -> x1, waiting for transfers between devices: none -> 26.5 us  [add_all(): parts = lax.all_gather(value, axis, axis=0, tiled=False)]
  transfers between devices with their start and end apart: 5 -> 5, of which waited for: 3 -> 3; matrix products, arithmetic and copies ran while one was open for 2% -> 3% of each run, Pallas kernels for 0% -> 0%
where the time goes in v1:
time: 120 us; the launch traced here: 119 us
  waiting for transfers between devices  35.4 us (30%)
  matrix products  24.5 us (20%)
  local copies, waits for them, and re-layouts  22.8 us (19%)
  starting transfers between devices  19.6 us (16%)
  between operations  13.5 us (11%)
  other arithmetic  3.61 us (3%)
    all_gather x1, waiting for transfers between devices, add_all(): parts = lax.all_gather(value, axis, axis=0, tiled=False)  26.5 us
    ppermute x4, starting transfers between devices, passed_along(): lax.ppermute(value, axis, [(i, (i + by) % length) for i in range(length)])  19.6 us
    unnamed x5, local copies, waits for them, and re-layouts  19.5 us
    dot_general x1, matrix products, per_device(): lax.dot_general(flat, flat, (((1,), (1,)), ((), ())), preferred_element_t...  12.9 us
    dot_general x1, matrix products, per_device(): jnp.einsum('mupl,mli->mupi', fit_blocks, picked, preferred_element_type=j...  11.6 us
    ppermute x4, waiting for transfers between devices, passed_along(): lax.ppermute(value, axis, [(i, (i + by) % length) for i in range(length)])  8.87 us
  transfers between devices with their start and end apart: 5, of which 3 were waited for; matrix products, arithmetic and copies ran while one was open for 3% of the time, Pallas kernels for 0%

profile of v1, /device:TPU:1, one launch (start us, length us, event | category | flops | bytes accessed | tf_op | source)
XLA Modules:
  0.0 119.4 jit_solution(2609976904088654832)
XLA Ops:
  6.5 0.0 all-gather.3.cloned.1.call-start
  6.5 3.7 %collective-permute-start = (bf16[256,512]{1,0:T(8,128)(2,1)}, bf16[256,512]{1,0:T(8,128)(2,1)S(1)}, u32[]{:S(2)}, u32[]{:S(2)}) collective-permute-start(bf16[256,512]{1,0:T(8,128)(2,1)} %param.5), channel_id=1, source_target_pairs={{0,4},{4,8},{8,12},{12,16},{16,20},{20,24},{24,28},{28,32},{32,36}... | collective-permute-start | bytes 786440 | tf_op jit(solution)/shard_map/ppermute | solution.py:15
  10.3 7.5 %collective-permute-start.2 = (bf16[256,512]{1,0:T(8,128)(2,1)}, bf16[256,512]{1,0:T(8,128)(2,1)S(1)}, u32[]{:S(2)}, u32[]{:S(2)}) collective-permute-start(bf16[256,512]{1,0:T(8,128)(2,1)} %param.5), channel_id=1, source_target_pairs={{0,252},{4,0},{8,4},{12,8},{16,12},{20,16},{24,20},{28,24},{32,28}... | collective-permute-start | bytes 786440 | tf_op jit(solution)/shard_map/ppermute | solution.py:15
  17.8 0.7 iota_compare_fusion
  18.5 0.7 compare_select_fusion
  19.2 4.8 %collective-permute-done = bf16[256,512]{1,0:T(8,128)(2,1)S(1)} collective-permute-done((bf16[256,512]{1,0:T(8,128)(2,1)}, bf16[256,512]{1,0:T(8,128)(2,1)S(1)}, u32[]{:S(2)}, u32[]{:S(2)}) %collective-permute-start) | collective-permute-done | bytes 262176 | tf_op jit(solution)/shard_map/ppermute | solution.py:15
  24.0 0.8 collective-permute-start.1
  24.8 0.7 fusion.8
  25.4 0.1 reshape.74
  25.5 0.1 broadcast_in_dim.23
  25.6 0.1 broadcast_in_dim.24
  25.7 0.0 collective-permute-done.2
  25.7 7.6 %collective-permute-start.3 = (bf16[256,512]{1,0:T(8,128)(2,1)S(1)}, bf16[256,512]{1,0:T(8,128)(2,1)S(1)}, u32[]{:S(2)}, u32[]{:S(2)}) collective-permute-start(bf16[256,512]{1,0:T(8,128)(2,1)S(1)} %collective-permute-done.2), channel_id=1, source_target_pairs={{0,252},{4,0},{8,4},{12,8},{16,12},{20,16},{24,20},{28,24},{32,28}... | collective-permute-start | bytes 786440 | tf_op jit(solution)/shard_map/ppermute | solution.py:15
  33.3 4.1 %collective-permute-done.1 = bf16[256,512]{1,0:T(8,128)(2,1)S(1)} collective-permute-done((bf16[256,512]{1,0:T(8,128)(2,1)S(1)}, bf16[256,512]{1,0:T(8,128)(2,1)S(1)}, u32[]{:S(2)}, u32[]{:S(2)}) %collective-permute-start.1) | collective-permute-done | bytes 262176 | tf_op jit(solution)/shard_map/ppermute | solution.py:15
  37.4 1.0 constant_dynamic-update-slice_fusion.2
  38.4 0.0 collective-permute-done.3
  38.4 0.6 gather_fusion
  39.1 0.2 bitcast_select_fusion
  39.3 11.6 %convolution_convert_fusion = bf16[4,512,64,64]{1,3,2,0:T(8,128)(2,1)} fusion(bf16[4,64,64,256]{3,2,1,0:T(8,128)(2,1)} %bitcast.31, bf16[4,256,512]{2,1,0:T(8,128)(2,1)S(1)} %bitcast_select_fusion), kind=kOutput, calls=%fused_computation.2 | convolution fusion | flops 4303355904 | bytes 26214400 | tf_op jit(solution)/shard_map/mupl,mli->mupi/dot_general | solution.py:48
  50.9 18.4 %copy.8 = bf16[32,8,64,512]{3,1,2,0:T(8,128)(2,1)} copy(bf16[32,8,64,512]{3,2,1,0:T(8,128)(2,1)} %bitcast.25) | data formatting | bytes 33554432
  69.3 12.9 %convolution_multiply_fusion = f32[256,256]{1,0:T(8,128)S(1)} fusion(bf16[256,32768]{1,0:T(8,128)(2,1)} %bitcast.26), kind=kOutput, calls=%fused_computation.3 | convolution fusion | flops 4295032832 | bytes 17039360 | tf_op jit(solution)/shard_map/dot_general | solution.py:53
  82.2 0.2 reshape.70
  82.5 0.1 copy.6
  82.6 0.2 reshape.71
  82.7 1.3 %gather_fusion.1 = f32[16,4096]{1,0:T(8,128)} fusion(f32[16,4096]{1,0:T(8,128)S(1)} %reshape.71, s32[1024]{0:T(1024)S(1)} %pad_clamp_fusion), kind=kCustom, calls=%fused_computation.1 | custom fusion | bytes 524352 | tf_op jit(solution)/shard_map/gather | solution.py:57
  84.1 0.0 all-gather.3.cloned.1.call-update
  84.1 26.5 %all-gather.3.cloned.1.call-done = f32[64,4096]{1,0:T(8,128)} async-done(((f32[16,4096]{1,0:T(8,128)}), f32[64,4096]{1,0:T(8,128)}) %all-gather.3.cloned.1.call-update) | async-done | bytes 1048592 | tf_op jit(solution)/shard_map/all_gather | solution.py:8
  110.6 1.3 %reduce_sum.9 = f32[16,4096]{1,0:T(8,128)S(1)} reduce(f32[4,16,4096]{2,1,0:T(8,128)} %bitcast.30, f32[]{:T(128)} %constant.68.clone.1), dimensions={0}, to_apply=%region_0.1 | reduce | flops 196608 | bytes 1310724 | tf_op jit(solution)/shard_map/reduce_sum | solution.py:9
  111.9 0.7 constant_dynamic-slice_fusion
  (6 shorter events, 0.1 us)
Async XLA Ops:
  6.5 104.0 %all-gather.3.cloned.1.call-start = ((), (), s32[]{:S(2)}) async-start(), calls=%async_computation | async-start | bytes 1310720 | tf_op jit(solution)/shard_map/all_gather | solution.py:8
  6.5 17.5 %collective-permute-start = (bf16[256,512]{1,0:T(8,128)(2,1)}, bf16[256,512]{1,0:T(8,128)(2,1)S(1)}, u32[]{:S(2)}, u32[]{:S(2)}) collective-permute-start(bf16[256,512]{1,0:T(8,128)(2,1)} %param.5), channel_id=1, source_target_pairs={{0,4},{4,8},{8,12},{12,16},{16,20},{20,24},{24,28},{28,32},{32,36}... | collective-permute-start | bytes 786440 | tf_op jit(solution)/shard_map/ppermute | solution.py:15
  10.3 15.4 %collective-permute-start.2 = (bf16[256,512]{1,0:T(8,128)(2,1)}, bf16[256,512]{1,0:T(8,128)(2,1)S(1)}, u32[]{:S(2)}, u32[]{:S(2)}) collective-permute-start(bf16[256,512]{1,0:T(8,128)(2,1)} %param.5), channel_id=1, source_target_pairs={{0,252},{4,0},{8,4},{12,8},{16,12},{20,16},{24,20},{28,24},{32,28}... | collective-permute-start | bytes 786440 | tf_op jit(solution)/shard_map/ppermute | solution.py:15
  24.0 13.3 %collective-permute-start.1 = (bf16[256,512]{1,0:T(8,128)(2,1)S(1)}, bf16[256,512]{1,0:T(8,128)(2,1)S(1)}, u32[]{:S(2)}, u32[]{:S(2)}) collective-permute-start(bf16[256,512]{1,0:T(8,128)(2,1)S(1)} %collective-permute-done), channel_id=1, source_target_pairs={{0,4},{4,8},{8,12},{12,16},{16,20},{20,24},{24,28},{28,32},{32,36}... | collective-permute-start | bytes 786440 | tf_op jit(solution)/shard_map/ppermute | solution.py:15
  25.7 12.7 %collective-permute-start.3 = (bf16[256,512]{1,0:T(8,128)(2,1)S(1)}, bf16[256,512]{1,0:T(8,128)(2,1)S(1)}, u32[]{:S(2)}, u32[]{:S(2)}) collective-permute-start(bf16[256,512]{1,0:T(8,128)(2,1)S(1)} %collective-permute-done.2), channel_id=1, source_target_pairs={{0,252},{4,0},{8,4},{12,8},{16,12},{20,16},{24,20},{28,24},{32,28}... | collective-permute-start | bytes 786440 | tf_op jit(solution)/shard_map/ppermute | solution.py:15
Sparse Core Ops, SparseCore 0:
  84.2 26.3 all-gather.2
